TPU v7x, 128 devices: a whole 4x4x4 slice. The times are simulated.
128 devices in a mesh: sx: 8 (over y, core), sy: 16 (over x, z).
Axes of the slice: x: 4, y: 4, z: 4, core: 2. Of those that a mesh axis runs over, the one named last changes fastest.
Arguments:
- loads: float32 [8, 16, 1536, 256], P('sx', 'sy')
- schur_flex: float32 [8, 16, 1536, 1536], P('sx', 'sy'), as said below
- dirichlet: float32 [8, 16, 1536, 1536], P('sx', 'sy'), as said below
- coupling: float32 [8, 16, 16, 1536], P('sx', 'sy'), may hold values from -0.3125 to 0.3125
- corner_index: int32 [8, 16, 16], P('sx', 'sy'), may hold values from 0 to 512, as said below
- face_lists: int32 [8, 16, 4, 384], P('sx', 'sy'), may hold values from 0 to 383, as said below
- coarse_inverse: float32 [512, 512], P(('sx', 'sy')), as said below
Outputs:
- multipliers: float32 [8, 16, 1536, 256], P('sx', 'sy')
- residual: float32 [8, 16, 1536, 256], P('sx', 'sy')
Inputs may be any that keep to these rules, and one draw needn't show every extreme that they name: `corner_index`: each subdomain lists 4 coarse dofs for each of its four corners; 512 marks a corner on the clamped edges of the panel, which has no coarse dof; every coarse dof below 512 is named by some subdomain. `face_lists`: each face's list is a permutation of the 384 dofs of the facing face; the facing lists of two neighbouring subdomains are inverse permutations. `schur_flex`: symmetric positive definite for every subdomain. `dirichlet`: symmetric positive definite for every subdomain. `coarse_inverse`: symmetric positive definite.
All inputs are finite; a program needn't handle non-finite values.
Results may differ from a plain program's by a relative error of at most 0.00017.
Values sent between devices are 32-bit elements; how exact they have to be, the bound alone decides.
A program may use at most 128 MiB of HBM per device.

v0:
```python
import jax
import jax.numpy as jnp
from jax import lax
from jax.sharding import PartitionSpec as P

ITERS = 2


def shifted(block, axis, distance):
    devices = range(lax.axis_size(axis))
    route = [(i - distance, i) for i in devices if i - distance in devices]
    return lax.ppermute(block, axis, route)


def jump(field, face_index):
    size = field.shape[0] // 4
    width = field.shape[1]
    face_rows = field.reshape(4, size, width)
    from_low_x = shifted(face_rows[1], "sx", 1)
    from_high_x = shifted(face_rows[0], "sx", -1)
    from_low_y = shifted(face_rows[3], "sy", 1)
    from_high_y = shifted(face_rows[2], "sy", -1)
    received = jnp.stack([from_low_x, from_high_x, from_low_y, from_high_y], axis=0)
    matched = received[jnp.arange(4, dtype=jnp.int32)[:, None], face_index]
    return (face_rows - matched).reshape(4 * size, width)


def coarse_solve(coarse_rhs, stiffness_inverse_lines):
    highest = lax.Precision.HIGHEST
    total = lax.psum(coarse_rhs, ("sx", "sy"))
    mine = jnp.dot(stiffness_inverse_lines, total, precision=highest)
    return lax.all_gather(mine, ("sx", "sy"), axis=0, tiled=True)


def inner(first, second):
    return jnp.sum(first * second, axis=0)


def shards(loads, schur_flex, dirichlet, coupling, corner_index, face_lists, coarse_inverse):
    high = lax.Precision.HIGH
    highest = lax.Precision.HIGHEST
    flex_mat = schur_flex[0, 0]
    prec_mat = dirichlet[0, 0]
    coupling_mat = coupling[0, 0]
    corners = corner_index[0, 0]
    face_index = face_lists[0, 0]
    ncoarse = coarse_inverse.shape[1]
    onehot = (corners[None, :] == jnp.arange(ncoarse, dtype=jnp.int32)[:, None]).astype(jnp.float32)
    size = face_index.shape[1]
    sx = lax.axis_index("sx")
    sy = lax.axis_index("sy")
    inside = jnp.stack([sx > 0, sx < lax.axis_size("sx") - 1, sy > 0, sy < lax.axis_size("sy") - 1])
    scale = jnp.repeat(1.0 + inside.astype(jnp.float32), size)[:, None]

    def total(values):
        return lax.psum(values, ("sx", "sy"))

    residual = jump(loads[0, 0], face_index)
    multipliers = jnp.zeros_like(residual)
    direction = None
    residual_inner = None
    for iteration in range(ITERS):
        spread = scale * residual
        operator_applied = jnp.dot(prec_mat, spread, precision=high)
        new_dot = total(0.5 * inner(spread, operator_applied))
        precond = 0.5 * jump(operator_applied, face_index)
        direction = precond if iteration == 0 else precond + new_dot / residual_inner * direction
        residual_inner = new_dot
        apply_spread = scale * direction
        fine_part = jnp.dot(flex_mat, apply_spread, precision=high)
        local_load = jnp.dot(coupling_mat, apply_spread, precision=high)
        coarse_rhs = jnp.dot(onehot, local_load, precision=highest)
        coarse_sol = coarse_solve(coarse_rhs, coarse_inverse)
        filled_out = jnp.concatenate(
            [coarse_sol, jnp.zeros((1, direction.shape[1]), jnp.float32)], axis=0
        )
        picked = filled_out[corners]
        correction = lax.dot_general(coupling_mat, picked, (((0,), (0,)), ((), ())), precision=high)
        applied = fine_part + correction
        step_size = residual_inner / total(inner(apply_spread, applied))
        image_dir = jump(applied, face_index)
        multipliers = multipliers + step_size * direction
        residual = residual - step_size * image_dir
    return (multipliers[None, None], residual[None, None])


def solution(mesh):
    return jax.shard_map(
        shards,
        mesh=mesh,
        in_specs=(
            P("sx", "sy", None, None),
            P("sx", "sy", None, None),
            P("sx", "sy", None, None),
            P("sx", "sy", None, None),
            P("sx", "sy", None),
            P("sx", "sy", None, None),
            P(("sx", "sy"), None),
        ),
        out_specs=(P("sx", "sy", None, None), P("sx", "sy", None, None)),
        check_vma=False,
    )
```

profile of v0, /device:TPU:1, one launch (start us, length us, event | category | flops | bytes accessed | tf_op | source)
XLA Modules:
  0.0 859.2 jit_solution(2950131900494569318)
XLA Ops:
  10.0 5.0 collective-permute-start.2
  17.9 3.2 collective-permute-start
  27.9 10.7 %gather_fusion = f32[1536,256]{1,0:T(8,128)S(1)} fusion(f32[4,384,256]{2,1,0:T(8,128)S(1)} %pad_maximum_fusion, s32[1536]{0:T(1024)S(1)} %reshape.131), kind=kCustom, calls=%fused_computation | custom fusion | bytes 3158016 | tf_op jit(solution)/shard_map/gather | solution.py:24
  38.6 11.8 %fusion.10 = f32[1536,256]{0,1:T(8,128)S(1)} fusion(f32[1,1,1536,1536]{3,2,1,0:T(8,128)} %param.9, f32[1,1,1536,256]{3,2,1,0:T(8,128)} %param.7, f32[1536,256]{1,0:T(8,128)S(1)} %gather_fusion, f32[1536]{0:T(1024)S(1)} %mul.105), kind=kOutput, calls=%fused_computation.19 | convolution fusion | flops 3624665088 | bytes 14161920 | tf_op jit(solution)/shard_map/dot_general | solution.py:64
  53.4 4.9 collective-permute-start.6
  60.2 4.8 collective-permute-start.4
  74.5 17.9 %gather_fusion.1 = f32[1536,256]{1,0:T(8,128)} fusion(f32[4,384,256]{2,1,0:T(8,128)S(1)} %copy.21, s32[1536]{0:T(1024)S(1)} %reshape.131), kind=kCustom, calls=%fused_computation.1 | custom fusion | bytes 3158016 | tf_op jit(solution)/shard_map/gather | solution.py:24
  92.4 3.1 copy.22
  100.6 6.7 fusion.2
  107.4 144.9 %all-reduce.6.cloned.1.call-done = f32[512,256]{1,0:T(8,128)} async-done(((f32[512,256]{1,0:T(8,128)}), f32[512,256]{1,0:T(8,128)}) %all-reduce.6.cloned.1.call-update) | async-done | bytes 524304 | tf_op jit(solution)/shard_map/psum | solution.py:30
  253.7 54.1 %all-gather = f32[128,4,256]{2,1,0:T(4,128)} all-gather(f32[1,4,256]{2,1,0:T(4,128)S(1)} %convolution_bitcast_fusion.1), channel_id=1, replica_groups=mesh['sx'=8,'sy'=16] {'sx','sy'}, dimensions={0}, use_global_device_ids=true | all-gather | bytes 528384 | tf_op jit(solution)/shard_map/all_gather | solution.py:32
  317.2 4.0 collective-permute-start.10
  323.7 3.1 collective-permute-start.8
  326.8 64.9 %all-reduce.2 = (f32[256]{0:T(256)S(1)}, f32[256]{0:T(256)S(1)}) all-reduce(f32[256]{0:T(256)S(1)} %broadcast_multiply_fusion.3, f32[256]{0:T(256)S(1)} %get-tuple-element.34), channel_id=1, replica_groups=mesh['sx'=8,'sy'=16] {'sx','sy'}, use_global_device_ids=true, to_apply=%region_1.0 | all-reduce | flops 512 | bytes 4096 | tf_op jit(solution)/shard_map/psum | solution.py:56
  396.0 17.9 %gather_fusion.3 = f32[1536,256]{1,0:T(8,128)} fusion(f32[4,384,256]{2,1,0:T(8,128)S(1)} %copy.25, s32[1536]{0:T(1024)S(1)} %reshape.131), kind=kCustom, calls=%fused_computation.3 | custom fusion | bytes 3158016 | tf_op jit(solution)/shard_map/gather | solution.py:24
  413.9 3.1 copy.26
  419.9 7.5 multiply_reduce_fusion.1
  430.2 4.0 collective-permute-start.14
  434.2 3.4 collective-permute-start.13
  439.8 65.1 %psum.45 = f32[256]{0:T(256)S(1)} all-reduce(f32[256]{0:T(256)S(1)} %broadcast_multiply_fusion.1), channel_id=1, replica_groups=mesh['sx'=8,'sy'=16] {'sx','sy'}, use_global_device_ids=true, to_apply=%region_6.0 | all-reduce | flops 256 | bytes 2048 | tf_op jit(solution)/shard_map/psum | solution.py:56
  509.3 17.9 %gather_fusion.4 = f32[1536,256]{1,0:T(8,128)} fusion(f32[4,384,256]{2,1,0:T(8,128)S(1)} %copy.27, s32[1536]{0:T(1024)S(1)} %reshape.131), kind=kCustom, calls=%fused_computation.4 | custom fusion | bytes 3158016 | tf_op jit(solution)/shard_map/gather | solution.py:24
  527.2 3.0 copy.28
  534.4 7.7 fusion
  542.2 134.3 %all-reduce.8.cloned.1.call-done = f32[512,256]{1,0:T(8,128)} async-done(((f32[512,256]{1,0:T(8,128)}), f32[512,256]{1,0:T(8,128)}) %all-reduce.8.cloned.1.call-update) | async-done | bytes 524304 | tf_op jit(solution)/shard_map/psum | solution.py:30
  677.9 54.1 %all-gather.1 = f32[128,4,256]{2,1,0:T(4,128)} all-gather(f32[1,4,256]{2,1,0:T(4,128)S(1)} %convolution_bitcast_fusion), channel_id=1, replica_groups=mesh['sx'=8,'sy'=16] {'sx','sy'}, dimensions={0}, use_global_device_ids=true | all-gather | bytes 528384 | tf_op jit(solution)/shard_map/all_gather | solution.py:32
  742.7 4.0 collective-permute-start.18
  749.2 3.1 collective-permute-start.16
  752.3 65.2 %psum.47 = f32[256]{0:T(256)S(1)} all-reduce(f32[256]{0:T(256)S(1)} %get-tuple-element.38), channel_id=1, replica_groups=mesh['sx'=8,'sy'=16] {'sx','sy'}, use_global_device_ids=true, to_apply=%region_9.0 | all-reduce | flops 256 | bytes 2048 | tf_op jit(solution)/shard_map/psum | solution.py:56
  821.8 17.9 %gather_fusion.6 = f32[1536,256]{1,0:T(8,128)} fusion(f32[4,384,256]{2,1,0:T(8,128)S(1)} %copy.29, s32[1536]{0:T(1024)S(1)} %reshape.131), kind=kCustom, calls=%fused_computation.6 | custom fusion | bytes 3158016 | tf_op jit(solution)/shard_map/gather | solution.py:24
  839.7 3.1 copy.30
  842.9 4.8 subtract_bitcast_fusion
  847.6 3.1 copy.31
  (117 shorter events, 85.9 us)
Async XLA Ops:
  7.2 91.2 %copy-start = (f32[1,1,16,1536]{3,2,1,0:T(8,128)S(1)}, f32[1,1,16,1536]{3,2,1,0:T(8,128)}, u32[]{:S(2)}) copy-start(f32[1,1,16,1536]{3,2,1,0:T(8,128)} %param.10) | copy-start | bytes 294916
  7.2 14.0 %copy-start.16 = (s32[1,1,4,384]{3,2,1,0:T(4,128)S(1)}, s32[1,1,4,384]{3,2,1,0:T(4,128)}, u32[]{:S(2)}) copy-start(s32[1,1,4,384]{3,2,1,0:T(4,128)} %param.12) | copy-start | bytes 18436
  7.2 245.1 %all-reduce.6.cloned.1.call-start = ((), (), s32[]{:S(2)}) async-start(), calls=%async_computation | async-start | bytes 1048576 | tf_op jit(solution)/shard_map/psum | solution.py:30
  8.7 13.2 %collective-permute-start.3 = (f32[384,256]{1,0:T(8,128)S(1)}, f32[384,256]{1,0:T(8,128)S(1)}, u32[]{:S(2)}, u32[]{:S(2)}) collective-permute-start(f32[384,256]{1,0:T(8,128)S(1)} %get-tuple-element.29), channel_id=1, source_target_pairs={{1,0},{2,1},{3,2},{4,3},{5,4},{6,5},{7,6},{8,7},{9,8},{10,9},{11,1... | collective-permute-start | bytes 1179656 | tf_op jit(solution)/shard_map/ppermute | solution.py:12
  10.0 12.8 %collective-permute-start.2 = (f32[384,256]{1,0:T(8,128)S(1)}, f32[384,256]{1,0:T(8,128)S(1)}, u32[]{:S(2)}, u32[]{:S(2)}) collective-permute-start(f32[384,256]{1,0:T(8,128)S(1)} %get-tuple-element.30), channel_id=1, source_target_pairs={{0,1},{1,2},{2,3},{3,4},{4,5},{5,6},{6,7},{7,8},{8,9},{9,10},{10,1... | collective-permute-start | bytes 1179656 | tf_op jit(solution)/shard_map/ppermute | solution.py:12
  15.0 9.6 %collective-permute-start.1 = (f32[384,256]{1,0:T(8,128)S(1)}, f32[384,256]{1,0:T(8,128)S(1)}, u32[]{:S(2)}, u32[]{:S(2)}) collective-permute-start(f32[384,256]{1,0:T(8,128)S(1)} %get-tuple-element.31), channel_id=1, source_target_pairs={{16,0},{32,16},{48,32},{64,48},{80,64},{96,80},{112,96},{17,1},{33... | collective-permute-start | bytes 1179656 | tf_op jit(solution)/shard_map/ppermute | solution.py:12
  17.9 7.9 collective-permute-start
  38.6 11.8 %copy-start.7 = (f32[1536,256]{1,0:T(8,128)}, f32[1536,256]{1,0:T(8,128)S(1)}, u32[]{:S(2)}) copy-start(f32[1536,256]{1,0:T(8,128)S(1)} %gather_fusion) | copy-start | bytes 4718596
  50.4 14.6 %copy-start.17 = (s32[1,1,16]{2,1,0:T(1,128)S(1)}, s32[1,1,16]{2,1,0:T(1,128)}, u32[]{:S(2)}) copy-start(s32[1,1,16]{2,1,0:T(1,128)} %param.11) | copy-start | bytes 196
  52.1 16.6 %collective-permute-start.7 = (f32[384,256]{0,1:T(8,128)}, f32[384,256]{0,1:T(8,128)}, u32[]{:S(2)}, u32[]{:S(2)}) collective-permute-start(f32[384,256]{0,1:T(8,128)} %get-tuple-element.25), channel_id=1, source_target_pairs={{1,0},{2,1},{3,2},{4,3},{5,4},{6,5},{7,6},{8,7},{9,8},{10,9},{11,1... | collective-permute-start | bytes 1179656 | tf_op jit(solution)/shard_map/ppermute | solution.py:12
  53.4 15.3 %collective-permute-start.6 = (f32[384,256]{0,1:T(8,128)}, f32[384,256]{0,1:T(8,128)}, u32[]{:S(2)}, u32[]{:S(2)}) collective-permute-start(f32[384,256]{0,1:T(8,128)} %get-tuple-element.26), channel_id=1, source_target_pairs={{0,1},{1,2},{2,3},{3,4},{4,5},{5,6},{6,7},{7,8},{8,9},{9,10},{10,1... | collective-permute-start | bytes 1179656 | tf_op jit(solution)/shard_map/ppermute | solution.py:12
  58.3 10.5 %collective-permute-start.5 = (f32[384,256]{0,1:T(8,128)}, f32[384,256]{0,1:T(8,128)}, u32[]{:S(2)}, u32[]{:S(2)}) collective-permute-start(f32[384,256]{0,1:T(8,128)} %get-tuple-element.27), channel_id=1, source_target_pairs={{16,0},{32,16},{48,32},{64,48},{80,64},{96,80},{112,96},{17,1},{33... | collective-permute-start | bytes 1179656 | tf_op jit(solution)/shard_map/ppermute | solution.py:12
  60.2 9.8 %collective-permute-start.4 = (f32[384,256]{0,1:T(8,128)}, f32[384,256]{0,1:T(8,128)}, u32[]{:S(2)}, u32[]{:S(2)}) collective-permute-start(f32[384,256]{0,1:T(8,128)} %get-tuple-element.24), channel_id=1, source_target_pairs={{0,16},{16,32},{32,48},{48,64},{64,80},{80,96},{96,112},{1,17},{17... | collective-permute-start | bytes 1179656 | tf_op jit(solution)/shard_map/ppermute | solution.py:12
  67.0 28.4 %copy-start.3 = (f32[1,1,1536,256]{2,3,1,0:T(8,128)}, f32[1,1,1536,256]{2,3,1,0:T(8,128)S(1)}, u32[]{:S(2)}) copy-start(f32[1,1,1536,256]{2,3,1,0:T(8,128)S(1)} %copy.23) | copy-start | bytes 4718596
  100.4 151.9 %copy-start.15 = (f32[4,512]{1,0:T(4,128)S(1)}, f32[4,512]{1,0:T(4,128)}, u32[]{:S(2)}) copy-start(f32[4,512]{1,0:T(4,128)} %param.13) | copy-start | bytes 24580
  100.4 576.1 %all-reduce.8.cloned.1.call-start = ((), (), s32[]{:S(2)}) async-start(), calls=%async_computation.1 | async-start | bytes 1048576 | tf_op jit(solution)/shard_map/psum | solution.py:30
  315.9 75.8 %collective-permute-start.11 = (f32[384,256]{0,1:T(8,128)}, f32[384,256]{0,1:T(8,128)S(1)}, u32[]{:S(2)}, u32[]{:S(2)}) collective-permute-start(f32[384,256]{0,1:T(8,128)} %get-tuple-element.21), channel_id=1, source_target_pairs={{1,0},{2,1},{3,2},{4,3},{5,4},{6,5},{7,6},{8,7},{9,8},{10,9},{11,1... | collective-permute-start | bytes 1179656 | tf_op jit(solution)/shard_map/ppermute | solution.py:12
  317.2 74.5 %collective-permute-start.10 = (f32[384,256]{0,1:T(8,128)}, f32[384,256]{0,1:T(8,128)S(1)}, u32[]{:S(2)}, u32[]{:S(2)}) collective-permute-start(f32[384,256]{0,1:T(8,128)} %get-tuple-element.22), channel_id=1, source_target_pairs={{0,1},{1,2},{2,3},{3,4},{4,5},{5,6},{6,7},{7,8},{8,9},{9,10},{10,1... | collective-permute-start | bytes 1179656 | tf_op jit(solution)/shard_map/ppermute | solution.py:12
  321.2 70.5 %collective-permute-start.9 = (f32[384,256]{0,1:T(8,128)S(1)}, f32[384,256]{0,1:T(8,128)}, u32[]{:S(2)}, u32[]{:S(2)}) collective-permute-start(f32[384,256]{0,1:T(8,128)S(1)} %get-tuple-element.23), channel_id=1, source_target_pairs={{16,0},{32,16},{48,32},{64,48},{80,64},{96,80},{112,96},{17,1},{33... | collective-permute-start | bytes 1179656 | tf_op jit(solution)/shard_map/ppermute | solution.py:12
  323.7 68.0 %collective-permute-start.8 = (f32[384,256]{0,1:T(8,128)S(1)}, f32[384,256]{0,1:T(8,128)}, u32[]{:S(2)}, u32[]{:S(2)}) collective-permute-start(f32[384,256]{0,1:T(8,128)S(1)} %get-tuple-element.20), channel_id=1, source_target_pairs={{0,16},{16,32},{32,48},{48,64},{64,80},{80,96},{96,112},{1,17},{17... | collective-permute-start | bytes 1179656 | tf_op jit(solution)/shard_map/ppermute | solution.py:12
  413.9 3.1 copy-start.4
  419.9 7.6 copy-start.10
  428.9 76.0 %collective-permute-start.15 = (f32[384,256]{0,1:T(8,128)}, f32[384,256]{0,1:T(8,128)S(1)}, u32[]{:S(2)}, u32[]{:S(2)}) collective-permute-start(f32[384,256]{0,1:T(8,128)} %get-tuple-element.15), channel_id=1, source_target_pairs={{1,0},{2,1},{3,2},{4,3},{5,4},{6,5},{7,6},{8,7},{9,8},{10,9},{11,1... | collective-permute-start | bytes 1179656 | tf_op jit(solution)/shard_map/ppermute | solution.py:12
  430.2 74.7 %collective-permute-start.14 = (f32[384,256]{0,1:T(8,128)}, f32[384,256]{0,1:T(8,128)S(1)}, u32[]{:S(2)}, u32[]{:S(2)}) collective-permute-start(f32[384,256]{0,1:T(8,128)} %get-tuple-element.16), channel_id=1, source_target_pairs={{0,1},{1,2},{2,3},{3,4},{4,5},{5,6},{6,7},{7,8},{8,9},{9,10},{10,1... | collective-permute-start | bytes 1179656 | tf_op jit(solution)/shard_map/ppermute | solution.py:12
  434.2 70.7 %collective-permute-start.13 = (f32[384,256]{0,1:T(8,128)S(1)}, f32[384,256]{0,1:T(8,128)}, u32[]{:S(2)}, u32[]{:S(2)}) collective-permute-start(f32[384,256]{0,1:T(8,128)S(1)} %get-tuple-element.17), channel_id=1, source_target_pairs={{16,0},{32,16},{48,32},{64,48},{80,64},{96,80},{112,96},{17,1},{33... | collective-permute-start | bytes 1179656 | tf_op jit(solution)/shard_map/ppermute | solution.py:12
  437.6 67.3 %collective-permute-start.12 = (f32[384,256]{0,1:T(8,128)S(1)}, f32[384,256]{0,1:T(8,128)}, u32[]{:S(2)}, u32[]{:S(2)}) collective-permute-start(f32[384,256]{0,1:T(8,128)S(1)} %get-tuple-element.14), channel_id=1, source_target_pairs={{0,16},{16,32},{32,48},{48,64},{64,80},{80,96},{96,112},{1,17},{17... | collective-permute-start | bytes 1179656 | tf_op jit(solution)/shard_map/ppermute | solution.py:12
  532.4 205.1 %copy-start.1 = (f32[1536,256]{0,1:T(8,128)}, f32[1536,256]{0,1:T(8,128)S(1)}, u32[]{:S(2)}) copy-start(f32[1536,256]{0,1:T(8,128)S(1)} %multiply_add_fusion) | copy-start | bytes 4718596
  741.4 76.0 %collective-permute-start.19 = (f32[384,256]{0,1:T(8,128)}, f32[384,256]{0,1:T(8,128)S(1)}, u32[]{:S(2)}, u32[]{:S(2)}) collective-permute-start(f32[384,256]{0,1:T(8,128)} %get-tuple-element.11), channel_id=1, source_target_pairs={{1,0},{2,1},{3,2},{4,3},{5,4},{6,5},{7,6},{8,7},{9,8},{10,9},{11,1... | collective-permute-start | bytes 1179656 | tf_op jit(solution)/shard_map/ppermute | solution.py:12
  742.7 74.8 %collective-permute-start.18 = (f32[384,256]{0,1:T(8,128)}, f32[384,256]{0,1:T(8,128)S(1)}, u32[]{:S(2)}, u32[]{:S(2)}) collective-permute-start(f32[384,256]{0,1:T(8,128)} %get-tuple-element.12), channel_id=1, source_target_pairs={{0,1},{1,2},{2,3},{3,4},{4,5},{5,6},{6,7},{7,8},{8,9},{9,10},{10,1... | collective-permute-start | bytes 1179656 | tf_op jit(solution)/shard_map/ppermute | solution.py:12
  746.7 70.7 %collective-permute-start.17 = (f32[384,256]{0,1:T(8,128)S(1)}, f32[384,256]{0,1:T(8,128)}, u32[]{:S(2)}, u32[]{:S(2)}) collective-permute-start(f32[384,256]{0,1:T(8,128)S(1)} %get-tuple-element.13), channel_id=1, source_target_pairs={{16,0},{32,16},{48,32},{64,48},{80,64},{96,80},{112,96},{17,1},{33... | collective-permute-start | bytes 1179656 | tf_op jit(solution)/shard_map/ppermute | solution.py:12
  749.2 68.3 %collective-permute-start.16 = (f32[384,256]{0,1:T(8,128)S(1)}, f32[384,256]{0,1:T(8,128)}, u32[]{:S(2)}, u32[]{:S(2)}) collective-permute-start(f32[384,256]{0,1:T(8,128)S(1)} %get-tuple-element.10), channel_id=1, source_target_pairs={{0,16},{16,32},{32,48},{48,64},{64,80},{80,96},{96,112},{1,17},{17... | collective-permute-start | bytes 1179656 | tf_op jit(solution)/shard_map/ppermute | solution.py:12
  847.6 3.1 copy-start.12
  (8 other events, 13.0 us)
Sparse Core Ops, SparseCore 0:
  100.5 151.7 all-reduce.5
  534.6 141.8 all-reduce.7
where the time goes:
time: 861 us; the launch traced here: 859 us
  blocking collectives  303 us (35%)
  waiting for transfers between devices  285 us (33%)
  local copies, waits for them, and re-layouts  130 us (15%)
  starting transfers between devices  58.1 us (7%)
  matrix products  44.1 us (5%)
  other arithmetic  24 us (3%)
  between operations  14.6 us (2%)
    psum x2, waiting for transfers between devices, coarse_solve(): total = lax.psum(coarse_rhs, ('sx', 'sy'))  279 us
    psum x3, blocking collectives, total(): return lax.psum(values, ('sx', 'sy'))  195 us
    all_gather x2, blocking collectives, coarse_solve(): return lax.all_gather(mine, ('sx', 'sy'), axis=0, tiled=True)  108 us
    gather x10, local copies, waits for them, and re-layouts, jump(): matched = received[jnp.arange(4, dtype=jnp.int32)[:, None], face_index]  96.4 us
    ppermute x20, starting transfers between devices, shifted(): return lax.ppermute(block, axis, route)  57.8 us
    dot_general x2, matrix products, shards(): operator_applied = jnp.dot(prec_mat, spread, precision=high)  19.4 us
  transfers between devices with their start and end apart: 22, of which 8 were waited for; matrix products, arithmetic and copies ran while one was open for 2% of the time, Pallas kernels for 0%

commit v1 on v0

--- a/solution.py
+++ b/solution.py
@@ -29,7 +29,9 @@
     highest = lax.Precision.HIGHEST
     total = lax.psum(coarse_rhs, ("sx", "sy"))
     mine = jnp.dot(stiffness_inverse_lines, total, precision=highest)
-    return lax.all_gather(mine, ("sx", "sy"), axis=0, tiled=True)
+    return jnp.concatenate(
+        lax.all_to_all(jnp.stack([mine] * lax.axis_size(("sx", "sy"))), ("sx", "sy"), 0, 0), axis=0
+    )
 
 
 def inner(first, second):

time: 861 us -> 796 us (0.925)
  blocking collectives: 303 us -> 195 us
  waiting for transfers between devices: 285 us -> 312 us
  starting transfers between devices: 58.1 us -> 73.4 us
    all_gather x2 -> x0, blocking collectives: 108 us -> none  [coarse_solve(): return lax.all_gather(mine, ('sx', 'sy'), axis=0, tiled=True)]
    psum x2, waiting for transfers between devices: 279 us -> 294 us  [coarse_solve(): total = lax.psum(coarse_rhs, ('sx', 'sy'))]
    all_to_all x0 -> x2, starting transfers between devices: none -> 14.5 us  [coarse_solve(): lax.all_to_all(jnp.stack([mine] * lax.axis_size(('sx', 'sy'))), ('sx', 's...]
    all_to_all x0 -> x2, waiting for transfers between devices: none -> 11.4 us  [coarse_solve(): lax.all_to_all(jnp.stack([mine] * lax.axis_size(('sx', 'sy'))), ('sx', 's...]
  transfers between devices with their start and end apart: 22 -> 24, of which waited for: 8 -> 10; matrix products, arithmetic and copies ran while one was open for 2% -> 2% of each run, Pallas kernels for 0% -> 0%
where the time goes in v1:
time: 796 us; the launch traced here: 794 us
  waiting for transfers between devices  312 us (39%)
  blocking collectives  195 us (24%)
  local copies, waits for them, and re-layouts  132 us (17%)
  starting transfers between devices  73.4 us (9%)
  matrix products  44.1 us (6%)
  other arithmetic  24 us (3%)
  between operations  14.6 us (2%)
    psum x2, waiting for transfers between devices, coarse_solve(): total = lax.psum(coarse_rhs, ('sx', 'sy'))  294 us
    psum x3, blocking collectives, total(): return lax.psum(values, ('sx', 'sy'))  195 us
    gather x10, local copies, waits for them, and re-layouts, jump(): matched = received[jnp.arange(4, dtype=jnp.int32)[:, None], face_index]  96.4 us
    ppermute x20, starting transfers between devices, shifted(): return lax.ppermute(block, axis, route)  58.6 us
    dot_general x2, matrix products, shards(): operator_applied = jnp.dot(prec_mat, spread, precision=high)  19.4 us
  transfers between devices with their start and end apart: 24, of which 10 were waited for; matrix products, arithmetic and copies ran while one was open for 2% of the time, Pallas kernels for 0%

profile of v1, /device:TPU:1, one launch (start us, length us, event | category | flops | bytes accessed | tf_op | source)
XLA Modules:
  0.0 794.0 jit_solution(6499109192745056895)
XLA Ops:
  10.0 5.0 collective-permute-start.2
  17.9 3.2 collective-permute-start
  27.9 10.7 %gather_fusion = f32[1536,256]{1,0:T(8,128)S(1)} fusion(f32[4,384,256]{2,1,0:T(8,128)S(1)} %pad_maximum_fusion, s32[1536]{0:T(1024)S(1)} %reshape.143), kind=kCustom, calls=%fused_computation | custom fusion | bytes 3158016 | tf_op jit(solution)/shard_map/gather | solution.py:24
  38.6 11.8 %fusion.10 = f32[1536,256]{0,1:T(8,128)S(1)} fusion(f32[1,1,1536,1536]{3,2,1,0:T(8,128)} %param.9, f32[1,1,1536,256]{3,2,1,0:T(8,128)} %param.7, f32[1536,256]{1,0:T(8,128)S(1)} %gather_fusion, f32[1536]{0:T(1024)S(1)} %mul.105), kind=kOutput, calls=%fused_computation.19 | convolution fusion | flops 3624665088 | bytes 14161920 | tf_op jit(solution)/shard_map/dot_general | solution.py:66
  53.4 4.9 collective-permute-start.6
  60.2 4.9 collective-permute-start.4
  74.6 18.0 %gather_fusion.1 = f32[1536,256]{1,0:T(8,128)} fusion(f32[4,384,256]{2,1,0:T(8,128)S(1)} %copy.9, s32[1536]{0:T(1024)S(1)} %reshape.143), kind=kCustom, calls=%fused_computation.1 | custom fusion | bytes 3158016 | tf_op jit(solution)/shard_map/gather | solution.py:24
  100.6 151.8 %all-reduce.6.cloned.1.call-done = f32[512,256]{1,0:T(8,128)} async-done(((f32[512,256]{1,0:T(8,128)}), f32[512,256]{1,0:T(8,128)}) %all-reduce.6.cloned.1.call-update) | async-done | bytes 524304 | tf_op jit(solution)/shard_map/psum | solution.py:30
  254.8 7.2 all-to-all-start
  262.2 6.7 fusion.2
  269.0 6.1 all-to-all-done
  284.4 4.0 collective-permute-start.10
  288.5 3.7 collective-permute-start.9
  294.4 64.6 %all-reduce.2 = (f32[256]{0:T(256)S(1)}, f32[256]{0:T(256)S(1)}) all-reduce(f32[256]{0:T(256)S(1)} %broadcast_multiply_fusion.3, f32[256]{0:T(256)S(1)} %get-tuple-element.32), channel_id=1, replica_groups=mesh['sx'=8,'sy'=16] {'sx','sy'}, use_global_device_ids=true, to_apply=%region_1.0 | all-reduce | flops 512 | bytes 4096 | tf_op jit(solution)/shard_map/psum | solution.py:58
  363.3 17.9 %gather_fusion.3 = f32[1536,256]{1,0:T(8,128)} fusion(f32[4,384,256]{2,1,0:T(8,128)S(1)} %copy.13, s32[1536]{0:T(1024)S(1)} %reshape.143), kind=kCustom, calls=%fused_computation.3 | custom fusion | bytes 3158016 | tf_op jit(solution)/shard_map/gather | solution.py:24
  381.2 3.1 copy.14
  387.2 7.5 multiply_reduce_fusion.1
  397.5 4.0 collective-permute-start.14
  401.5 3.4 collective-permute-start.13
  407.1 65.1 %psum.45 = f32[256]{0:T(256)S(1)} all-reduce(f32[256]{0:T(256)S(1)} %broadcast_multiply_fusion.1), channel_id=1, replica_groups=mesh['sx'=8,'sy'=16] {'sx','sy'}, use_global_device_ids=true, to_apply=%region_6.0 | all-reduce | flops 256 | bytes 2048 | tf_op jit(solution)/shard_map/psum | solution.py:58
  476.6 18.0 %gather_fusion.4 = f32[1536,256]{1,0:T(8,128)} fusion(f32[4,384,256]{2,1,0:T(8,128)S(1)} %copy.15, s32[1536]{0:T(1024)S(1)} %reshape.143), kind=kCustom, calls=%fused_computation.4 | custom fusion | bytes 3158016 | tf_op jit(solution)/shard_map/gather | solution.py:24
  501.7 142.4 %all-reduce.8.cloned.1.call-done = f32[512,256]{1,0:T(8,128)} async-done(((f32[512,256]{1,0:T(8,128)}), f32[512,256]{1,0:T(8,128)}) %all-reduce.8.cloned.1.call-update) | async-done | bytes 524304 | tf_op jit(solution)/shard_map/psum | solution.py:30
  646.4 7.2 all-to-all-start.1
  653.6 7.7 fusion
  661.4 5.3 all-to-all-done.1
  677.4 4.0 collective-permute-start.18
  681.4 3.7 collective-permute-start.17
  687.4 64.9 %psum.47 = f32[256]{0:T(256)S(1)} all-reduce(f32[256]{0:T(256)S(1)} %get-tuple-element.36), channel_id=1, replica_groups=mesh['sx'=8,'sy'=16] {'sx','sy'}, use_global_device_ids=true, to_apply=%region_9.0 | all-reduce | flops 256 | bytes 2048 | tf_op jit(solution)/shard_map/psum | solution.py:58
  756.6 17.9 %gather_fusion.6 = f32[1536,256]{1,0:T(8,128)} fusion(f32[4,384,256]{2,1,0:T(8,128)S(1)} %copy.17, s32[1536]{0:T(1024)S(1)} %reshape.143), kind=kCustom, calls=%fused_computation.6 | custom fusion | bytes 3158016 | tf_op jit(solution)/shard_map/gather | solution.py:24
  774.5 3.1 copy.18
  777.6 4.8 subtract_bitcast_fusion
  782.4 3.1 copy.19
  (121 shorter events, 93.2 us)
Async XLA Ops:
  7.2 91.5 %copy-start = (f32[1,1,16,1536]{3,2,1,0:T(8,128)S(1)}, f32[1,1,16,1536]{3,2,1,0:T(8,128)}, u32[]{:S(2)}) copy-start(f32[1,1,16,1536]{3,2,1,0:T(8,128)} %param.10) | copy-start | bytes 294916
  7.2 14.0 %copy-start.16 = (s32[1,1,4,384]{3,2,1,0:T(4,128)S(1)}, s32[1,1,4,384]{3,2,1,0:T(4,128)}, u32[]{:S(2)}) copy-start(s32[1,1,4,384]{3,2,1,0:T(4,128)} %param.12) | copy-start | bytes 18436
  7.2 245.3 %all-reduce.6.cloned.1.call-start = ((), (), s32[]{:S(2)}) async-start(), calls=%async_computation.2 | async-start | bytes 1048576 | tf_op jit(solution)/shard_map/psum | solution.py:30
  8.7 13.2 %collective-permute-start.3 = (f32[384,256]{1,0:T(8,128)S(1)}, f32[384,256]{1,0:T(8,128)S(1)}, u32[]{:S(2)}, u32[]{:S(2)}) collective-permute-start(f32[384,256]{1,0:T(8,128)S(1)} %get-tuple-element.27), channel_id=1, source_target_pairs={{1,0},{2,1},{3,2},{4,3},{5,4},{6,5},{7,6},{8,7},{9,8},{10,9},{11,1... | collective-permute-start | bytes 1179656 | tf_op jit(solution)/shard_map/ppermute | solution.py:12
  10.0 12.8 %collective-permute-start.2 = (f32[384,256]{1,0:T(8,128)S(1)}, f32[384,256]{1,0:T(8,128)S(1)}, u32[]{:S(2)}, u32[]{:S(2)}) collective-permute-start(f32[384,256]{1,0:T(8,128)S(1)} %get-tuple-element.28), channel_id=1, source_target_pairs={{0,1},{1,2},{2,3},{3,4},{4,5},{5,6},{6,7},{7,8},{8,9},{9,10},{10,1... | collective-permute-start | bytes 1179656 | tf_op jit(solution)/shard_map/ppermute | solution.py:12
  15.0 9.6 %collective-permute-start.1 = (f32[384,256]{1,0:T(8,128)S(1)}, f32[384,256]{1,0:T(8,128)S(1)}, u32[]{:S(2)}, u32[]{:S(2)}) collective-permute-start(f32[384,256]{1,0:T(8,128)S(1)} %get-tuple-element.29), channel_id=1, source_target_pairs={{16,0},{32,16},{48,32},{64,48},{80,64},{96,80},{112,96},{17,1},{33... | collective-permute-start | bytes 1179656 | tf_op jit(solution)/shard_map/ppermute | solution.py:12
  17.9 7.9 collective-permute-start
  38.6 11.8 %copy-start.7 = (f32[1536,256]{1,0:T(8,128)}, f32[1536,256]{1,0:T(8,128)S(1)}, u32[]{:S(2)}) copy-start(f32[1536,256]{1,0:T(8,128)S(1)} %gather_fusion) | copy-start | bytes 4718596
  52.1 16.6 %collective-permute-start.7 = (f32[384,256]{0,1:T(8,128)}, f32[384,256]{0,1:T(8,128)}, u32[]{:S(2)}, u32[]{:S(2)}) collective-permute-start(f32[384,256]{0,1:T(8,128)} %get-tuple-element.23), channel_id=1, source_target_pairs={{1,0},{2,1},{3,2},{4,3},{5,4},{6,5},{7,6},{8,7},{9,8},{10,9},{11,1... | collective-permute-start | bytes 1179656 | tf_op jit(solution)/shard_map/ppermute | solution.py:12
  53.4 15.3 %collective-permute-start.6 = (f32[384,256]{0,1:T(8,128)}, f32[384,256]{0,1:T(8,128)}, u32[]{:S(2)}, u32[]{:S(2)}) collective-permute-start(f32[384,256]{0,1:T(8,128)} %get-tuple-element.24), channel_id=1, source_target_pairs={{0,1},{1,2},{2,3},{3,4},{4,5},{5,6},{6,7},{7,8},{8,9},{9,10},{10,1... | collective-permute-start | bytes 1179656 | tf_op jit(solution)/shard_map/ppermute | solution.py:12
  58.3 10.5 %collective-permute-start.5 = (f32[384,256]{0,1:T(8,128)}, f32[384,256]{0,1:T(8,128)}, u32[]{:S(2)}, u32[]{:S(2)}) collective-permute-start(f32[384,256]{0,1:T(8,128)} %get-tuple-element.25), channel_id=1, source_target_pairs={{16,0},{32,16},{48,32},{64,48},{80,64},{96,80},{112,96},{17,1},{33... | collective-permute-start | bytes 1179656 | tf_op jit(solution)/shard_map/ppermute | solution.py:12
  60.2 6.8 copy-start.8
  60.2 9.9 %collective-permute-start.4 = (f32[384,256]{0,1:T(8,128)}, f32[384,256]{0,1:T(8,128)}, u32[]{:S(2)}, u32[]{:S(2)}) collective-permute-start(f32[384,256]{0,1:T(8,128)} %get-tuple-element.22), channel_id=1, source_target_pairs={{0,16},{16,32},{32,48},{48,64},{64,80},{80,96},{96,112},{1,17},{17... | collective-permute-start | bytes 1179656 | tf_op jit(solution)/shard_map/ppermute | solution.py:12
  67.0 28.6 %copy-start.3 = (f32[1,1,1536,256]{2,3,1,0:T(8,128)}, f32[1,1,1536,256]{2,3,1,0:T(8,128)S(1)}, u32[]{:S(2)}) copy-start(f32[1,1,1536,256]{2,3,1,0:T(8,128)S(1)} %copy.11) | copy-start | bytes 4718596
  98.6 153.9 %copy-start.15 = (f32[4,512]{1,0:T(4,128)S(1)}, f32[4,512]{1,0:T(4,128)}, u32[]{:S(2)}) copy-start(f32[4,512]{1,0:T(4,128)} %param.13) | copy-start | bytes 24580
  254.8 20.3 %all-to-all-start = ((f32[128,4,256]{2,1,0:T(4,128)}), f32[128,4,256]{2,1,0:T(4,128)}, u32[]{:S(2)}, u32[]{:S(2)}) async-start(f32[128,4,256]{2,1,0:T(4,128)} %stack.79), calls=%async_computation | async-start | bytes 1048576 | tf_op jit(solution)/shard_map/all_to_all | solution.py:33
  262.0 382.1 %all-reduce.8.cloned.1.call-start = ((), (), s32[]{:S(2)}) async-start(), calls=%async_computation.3 | async-start | bytes 1048576 | tf_op jit(solution)/shard_map/psum | solution.py:30
  283.2 75.8 %collective-permute-start.11 = (f32[384,256]{0,1:T(8,128)}, f32[384,256]{0,1:T(8,128)S(1)}, u32[]{:S(2)}, u32[]{:S(2)}) collective-permute-start(f32[384,256]{0,1:T(8,128)} %get-tuple-element.19), channel_id=1, source_target_pairs={{1,0},{2,1},{3,2},{4,3},{5,4},{6,5},{7,6},{8,7},{9,8},{10,9},{11,1... | collective-permute-start | bytes 1179656 | tf_op jit(solution)/shard_map/ppermute | solution.py:12
  284.4 74.5 %collective-permute-start.10 = (f32[384,256]{0,1:T(8,128)}, f32[384,256]{0,1:T(8,128)S(1)}, u32[]{:S(2)}, u32[]{:S(2)}) collective-permute-start(f32[384,256]{0,1:T(8,128)} %get-tuple-element.20), channel_id=1, source_target_pairs={{0,1},{1,2},{2,3},{3,4},{4,5},{5,6},{6,7},{7,8},{8,9},{9,10},{10,1... | collective-permute-start | bytes 1179656 | tf_op jit(solution)/shard_map/ppermute | solution.py:12
  288.5 70.5 %collective-permute-start.9 = (f32[384,256]{0,1:T(8,128)S(1)}, f32[384,256]{0,1:T(8,128)}, u32[]{:S(2)}, u32[]{:S(2)}) collective-permute-start(f32[384,256]{0,1:T(8,128)S(1)} %get-tuple-element.21), channel_id=1, source_target_pairs={{16,0},{32,16},{48,32},{64,48},{80,64},{96,80},{112,96},{17,1},{33... | collective-permute-start | bytes 1179656 | tf_op jit(solution)/shard_map/ppermute | solution.py:12
  292.2 66.8 %collective-permute-start.8 = (f32[384,256]{0,1:T(8,128)S(1)}, f32[384,256]{0,1:T(8,128)}, u32[]{:S(2)}, u32[]{:S(2)}) collective-permute-start(f32[384,256]{0,1:T(8,128)S(1)} %get-tuple-element.18), channel_id=1, source_target_pairs={{0,16},{16,32},{32,48},{48,64},{64,80},{80,96},{96,112},{1,17},{17... | collective-permute-start | bytes 1179656 | tf_op jit(solution)/shard_map/ppermute | solution.py:12
  387.2 7.6 copy-start.10
  396.2 76.0 %collective-permute-start.15 = (f32[384,256]{0,1:T(8,128)}, f32[384,256]{0,1:T(8,128)S(1)}, u32[]{:S(2)}, u32[]{:S(2)}) collective-permute-start(f32[384,256]{0,1:T(8,128)} %get-tuple-element.13), channel_id=1, source_target_pairs={{1,0},{2,1},{3,2},{4,3},{5,4},{6,5},{7,6},{8,7},{9,8},{10,9},{11,1... | collective-permute-start | bytes 1179656 | tf_op jit(solution)/shard_map/ppermute | solution.py:12
  397.5 74.7 %collective-permute-start.14 = (f32[384,256]{0,1:T(8,128)}, f32[384,256]{0,1:T(8,128)S(1)}, u32[]{:S(2)}, u32[]{:S(2)}) collective-permute-start(f32[384,256]{0,1:T(8,128)} %get-tuple-element.14), channel_id=1, source_target_pairs={{0,1},{1,2},{2,3},{3,4},{4,5},{5,6},{6,7},{7,8},{8,9},{9,10},{10,1... | collective-permute-start | bytes 1179656 | tf_op jit(solution)/shard_map/ppermute | solution.py:12
  401.5 70.7 %collective-permute-start.13 = (f32[384,256]{0,1:T(8,128)S(1)}, f32[384,256]{0,1:T(8,128)}, u32[]{:S(2)}, u32[]{:S(2)}) collective-permute-start(f32[384,256]{0,1:T(8,128)S(1)} %get-tuple-element.15), channel_id=1, source_target_pairs={{16,0},{32,16},{48,32},{64,48},{80,64},{96,80},{112,96},{17,1},{33... | collective-permute-start | bytes 1179656 | tf_op jit(solution)/shard_map/ppermute | solution.py:12
  404.9 67.3 %collective-permute-start.12 = (f32[384,256]{0,1:T(8,128)S(1)}, f32[384,256]{0,1:T(8,128)}, u32[]{:S(2)}, u32[]{:S(2)}) collective-permute-start(f32[384,256]{0,1:T(8,128)S(1)} %get-tuple-element.12), channel_id=1, source_target_pairs={{0,16},{16,32},{32,48},{48,64},{64,80},{80,96},{96,112},{1,17},{17... | collective-permute-start | bytes 1179656 | tf_op jit(solution)/shard_map/ppermute | solution.py:12
  499.8 172.5 %copy-start.1 = (f32[1536,256]{0,1:T(8,128)}, f32[1536,256]{0,1:T(8,128)S(1)}, u32[]{:S(2)}) copy-start(f32[1536,256]{0,1:T(8,128)S(1)} %multiply_add_fusion) | copy-start | bytes 4718596
  646.4 20.3 %all-to-all-start.1 = ((f32[128,4,256]{2,1,0:T(4,128)}), f32[128,4,256]{2,1,0:T(4,128)}, u32[]{:S(2)}, u32[]{:S(2)}) async-start(f32[128,4,256]{2,1,0:T(4,128)} %stack.90), calls=%async_computation.1 | async-start | bytes 1048576 | tf_op jit(solution)/shard_map/all_to_all | solution.py:33
  676.1 76.1 %collective-permute-start.19 = (f32[384,256]{0,1:T(8,128)}, f32[384,256]{0,1:T(8,128)S(1)}, u32[]{:S(2)}, u32[]{:S(2)}) collective-permute-start(f32[384,256]{0,1:T(8,128)} %get-tuple-element.9), channel_id=1, source_target_pairs={{1,0},{2,1},{3,2},{4,3},{5,4},{6,5},{7,6},{8,7},{9,8},{10,9},{11,1... | collective-permute-start | bytes 1179656 | tf_op jit(solution)/shard_map/ppermute | solution.py:12
  677.4 74.8 %collective-permute-start.18 = (f32[384,256]{0,1:T(8,128)}, f32[384,256]{0,1:T(8,128)S(1)}, u32[]{:S(2)}, u32[]{:S(2)}) collective-permute-start(f32[384,256]{0,1:T(8,128)} %get-tuple-element.10), channel_id=1, source_target_pairs={{0,1},{1,2},{2,3},{3,4},{4,5},{5,6},{6,7},{7,8},{8,9},{9,10},{10,1... | collective-permute-start | bytes 1179656 | tf_op jit(solution)/shard_map/ppermute | solution.py:12
  681.4 70.8 %collective-permute-start.17 = (f32[384,256]{0,1:T(8,128)S(1)}, f32[384,256]{0,1:T(8,128)}, u32[]{:S(2)}, u32[]{:S(2)}) collective-permute-start(f32[384,256]{0,1:T(8,128)S(1)} %get-tuple-element.11), channel_id=1, source_target_pairs={{16,0},{32,16},{48,32},{64,48},{80,64},{96,80},{112,96},{17,1},{33... | collective-permute-start | bytes 1179656 | tf_op jit(solution)/shard_map/ppermute | solution.py:12
  685.2 67.1 %collective-permute-start.16 = (f32[384,256]{0,1:T(8,128)S(1)}, f32[384,256]{0,1:T(8,128)}, u32[]{:S(2)}, u32[]{:S(2)}) collective-permute-start(f32[384,256]{0,1:T(8,128)S(1)} %get-tuple-element.8), channel_id=1, source_target_pairs={{0,16},{16,32},{32,48},{48,64},{64,80},{80,96},{96,112},{1,17},{17... | collective-permute-start | bytes 1179656 | tf_op jit(solution)/shard_map/ppermute | solution.py:12
  (10 other events, 18.0 us)
Sparse Core Ops, SparseCore 0:
  100.7 151.7 all-reduce.5
  501.8 142.2 all-reduce.7
